TPU v7x, 32 devices: a whole 2x2x4 slice. The times are simulated.
32 devices in a mesh: row: 8 (over y, x, core), col: 4 (over z).
Axes of the slice: x: 2, y: 2, z: 4, core: 2. Of those that a mesh axis runs over, the one named last changes fastest.
Arguments:
- inputs: bfloat16 [1024, 6144], P('row', 'col'), may hold values from -6 to 6
- up_cells: int32 [4, 576], P('col'), may hold values from 0 to 2303, as said below
- up_blocks: bfloat16 [4, 576, 128, 128], P('col', 'row'), may hold values from -0.15625 to 0.15625
- down_cells: int32 [4, 576], P('col'), may hold values from 0 to 2303, as said below
- down_blocks: bfloat16 [4, 576, 128, 128], P('col', 'row'), may hold values from -0.078125 to 0.078125
- cotangent: bfloat16 [1024, 6144], P('row', 'col'), may hold values from -6 to 6
Outputs:
- output: bfloat16 [1024, 6144], P('row', 'col')
- input_grad: bfloat16 [1024, 6144], P('row', 'col')
- up_grad: bfloat16 [4, 576, 128, 128], P('col', 'row')
- down_grad: bfloat16 [4, 576, 128, 128], P('col', 'row')
Inputs may be any that keep to these rules, and one draw needn't show every extreme that they name: Each row of up_cells names 576 distinct block numbers of its panel. Each row of down_cells names 576 distinct block numbers of its panel.
All inputs are finite; a program needn't handle non-finite values.
Results may differ from a plain program's by a relative error of at most 0.012.
Values may be sent and summed in bfloat16 or wider, within the bound.
No kernel may reach another device: no remote copies, remote signals or barrier semaphores. Data moves between devices by JAX's collectives and lax.ppermute only.
A program may use at most 192 MiB of HBM per device.

v0:
```python
import math

import jax
import jax.numpy as jnp
from jax import lax
from jax.sharding import PartitionSpec as P

D = 6144
H = 24576


def pick_blocks(tiles, numbers):
    onehot = (numbers[:, None] == jnp.arange(tiles.shape[1], dtype=jnp.int32)[None, :]).astype(
        tiles.dtype
    )
    picked = jnp.einsum("tcb,nc->tnb", tiles, onehot, preferred_element_type=jnp.float32)
    return picked.astype(tiles.dtype)


def place_add(running, product, targets):
    onehot = (targets[:, None] == jnp.arange(running.shape[1], dtype=jnp.int32)[None, :]).astype(
        jnp.float32
    )
    return running + jnp.einsum("tnj,nc->tcj", product, onehot, precision=lax.Precision.HIGHEST)


def run_groups(running, blocks, numbers, per_dev, step_fn):
    side_len = blocks.shape[-1]
    grouped_blocks = blocks.reshape(-1, per_dev, side_len, side_len)
    grouped_numbers = numbers.reshape(-1, per_dev)

    def inner(state, element):
        return (step_fn(state, element[0], element[1]), None)

    result, _ = lax.scan(inner, running, (grouped_blocks, grouped_numbers))
    return result


def shards(inputs, up_cells, up_blocks, down_cells, down_blocks, cotangent):
    per_dev = up_blocks.shape[1]
    side_len = up_blocks.shape[-1]
    rows_here = inputs.shape[0]
    in_blocks = D // side_len
    hid_blocks = H // (side_len * lax.axis_size("col"))
    factor = 1.0 / math.sqrt(rows_here * lax.axis_size("row"))
    inputs_all, cotan_all = (
        lax.all_gather(inputs, "col", axis=1, tiled=True),
        lax.all_gather(cotangent, "col", axis=1, tiled=True),
    )
    in_tiles = inputs_all.reshape(rows_here, in_blocks, side_len)
    cot_tiles = cotan_all.reshape(rows_here, in_blocks, side_len)
    list_up = up_cells[0]
    list_down = down_cells[0]

    def up_step(running, blocks, numbers):
        taken = pick_blocks(in_tiles, numbers // hid_blocks)
        product = jnp.einsum("tnk,nkj->tnj", taken, blocks, preferred_element_type=jnp.float32)
        return place_add(running, product, numbers % hid_blocks)

    hid_zero = jnp.zeros((rows_here, hid_blocks, side_len), jnp.float32)
    feat_zero = jnp.zeros((rows_here, in_blocks, side_len), jnp.float32)
    numbers = list_up
    preact = run_groups(
        hid_zero, lax.all_gather(up_blocks, "row", axis=1, tiled=True)[0], numbers, per_dev, up_step
    )
    sigmoid_val = jax.nn.sigmoid(preact)
    hidden = (preact * sigmoid_val).astype(jnp.bfloat16)
    derivative = sigmoid_val * (1.0 + preact * (1.0 - sigmoid_val))

    def down_step(running, blocks, numbers):
        source = numbers // in_blocks
        target = numbers % in_blocks
        hid_taken = pick_blocks(hidden, source)
        forward = jnp.einsum("tnk,nkj->tnj", hid_taken, blocks, preferred_element_type=jnp.float32)
        cot_taken = pick_blocks(cot_tiles, target)
        backward = jnp.einsum("tnj,nkj->tnk", cot_taken, blocks, preferred_element_type=jnp.float32)
        return (place_add(running[0], forward, target), place_add(running[1], backward, source))

    numbers = list_down
    out_partial, hidden_grad = run_groups(
        (feat_zero, hid_zero),
        lax.all_gather(down_blocks, "row", axis=1, tiled=True)[0],
        numbers,
        per_dev,
        down_step,
    )
    output = lax.psum_scatter(
        out_partial.reshape(rows_here, D).astype(jnp.bfloat16),
        "col",
        scatter_dimension=1,
        tiled=True,
    )
    act_grad = (hidden_grad * derivative).astype(jnp.bfloat16)
    numbers = list_down.reshape(-1, per_dev)

    def down_group_term(chosen):
        lhs_rows = pick_blocks(hidden, chosen // in_blocks)
        rhs_rows = pick_blocks(cot_tiles, chosen % in_blocks)
        return (
            jnp.einsum("tnk,tnj->nkj", lhs_rows, rhs_rows, preferred_element_type=jnp.float32)
            * factor
        )

    down_sum = lax.psum_scatter(
        lax.map(down_group_term, numbers)
        .reshape(per_dev * lax.axis_size("row"), side_len, side_len)
        .astype(jnp.bfloat16),
        "row",
        scatter_dimension=0,
        tiled=True,
    )

    def back_step(running, blocks, numbers):
        act_taken = pick_blocks(act_grad, numbers % hid_blocks)
        product = jnp.einsum("tnj,nkj->tnk", act_taken, blocks, preferred_element_type=jnp.float32)
        return place_add(running, product, numbers // hid_blocks)

    numbers = list_up
    in_partial = run_groups(
        feat_zero,
        lax.all_gather(up_blocks, "row", axis=1, tiled=True)[0],
        numbers,
        per_dev,
        back_step,
    )
    input_grad = lax.psum_scatter(
        in_partial.reshape(rows_here, D).astype(jnp.bfloat16),
        "col",
        scatter_dimension=1,
        tiled=True,
    )
    numbers = list_up.reshape(-1, per_dev)

    def up_group_term(chosen):
        lhs_rows = pick_blocks(in_tiles, chosen // hid_blocks)
        rhs_rows = pick_blocks(act_grad, chosen % hid_blocks)
        return (
            jnp.einsum("tnk,tnj->nkj", lhs_rows, rhs_rows, preferred_element_type=jnp.float32)
            * factor
        )

    up_sum = lax.psum_scatter(
        lax.map(up_group_term, numbers)
        .reshape(per_dev * lax.axis_size("row"), side_len, side_len)
        .astype(jnp.bfloat16),
        "row",
        scatter_dimension=0,
        tiled=True,
    )
    up_grad = up_sum.reshape(1, per_dev, side_len, side_len)
    down_grad = down_sum.reshape(1, per_dev, side_len, side_len)
    return (output, input_grad, up_grad, down_grad)


def solution(mesh):
    in_specs = (
        P("row", "col"),
        P("col", None),
        P("col", "row", None, None),
        P("col", None),
        P("col", "row", None, None),
        P("row", "col"),
    )
    out_specs = (
        P("row", "col"),
        P("row", "col"),
        P("col", "row", None, None),
        P("col", "row", None, None),
    )
    return jax.shard_map(shards, mesh=mesh, in_specs=in_specs, out_specs=out_specs, check_vma=False)
```

profile of v0, /device:TPU:0, one launch (start us, length us, event | category | flops | bytes accessed | tf_op | source)
XLA Modules:
  0.0 1199.0 jit_solution(8238825209214660622)
XLA Ops:
  10.3 39.1 %all-gather.9.cloned.1.call-done = bf16[128,6144]{1,0:T(8,128)(2,1)} async-done(((bf16[128,1536]{1,0:T(8,128)(2,1)}), bf16[128,6144]{1,0:T(8,128)(2,1)}) %all-gather.9.cloned.1.call-update) | async-done | bytes 1572880 | tf_op jit(solution)/shard_map/all_gather | solution.py:47
  51.1 35.7 %all-gather.11.cloned.1.call-done = bf16[128,6144]{1,0:T(8,128)(2,1)} async-done(((bf16[128,1536]{1,0:T(8,128)(2,1)}), bf16[128,6144]{1,0:T(8,128)(2,1)}) %all-gather.11.cloned.1.call-update) | async-done | bytes 1572880 | tf_op jit(solution)/shard_map/all_gather | solution.py:48
  88.6 97.6 %all-gather.7.cloned.1.call-done = bf16[1,576,128,128]{3,2,0,1:T(8,128)(2,1)} async-done(((bf16[1,72,128,128]{3,2,0,1:T(8,128)(2,1)}), bf16[1,576,128,128]{3,2,0,1:T(8,128)(2,1)}) %all-gather.7.cloned.1.call-update) | async-done | bytes 18874384 | tf_op jit(solution)/shard_map/all_gather | solution.py:64
  186.2 161.4 %while.67 = (s32[]{:T(128)}, f32[128,48,128]{2,1,0:T(8,128)}, s32[8,72]{1,0:T(8,128)S(1)}, bf16[8,72,128,128]{3,2,1,0:T(8,128)(2,1)}, bf16[128,48,128]{2,1,0:T(8,128)(2,1)S(1)}, /*index=5*/s32[]{:T(128)}, s32[]{:T(128)}) while((s32[]{:T(128)}, f32[128,48,128]{2,1,0:T(8,128)}, s32[8,72]{1,0:T(8,128)S(1)}, ...), condition=%wide.region_1.2_spmd.clone, body=%wide.region_0.1_spmd.clone.sunk | while | flops 1096294016 | bytes 33818116 | solution.py:35
  218.6 7.4 bitcast_add_fusion.8
  239.7 7.5 bitcast_add_fusion.8
  259.9 7.4 bitcast_add_fusion.8
  280.0 7.4 bitcast_add_fusion.8
  300.0 7.4 bitcast_add_fusion.8
  320.1 7.4 bitcast_add_fusion.8
  340.2 7.4 bitcast_add_fusion.8
  351.5 318.6 %while.68 = (s32[]{:T(128)}, f32[128,48,128]{2,1,0:T(8,128)}, f32[128,48,128]{2,1,0:T(8,128)}, s32[8,72]{1,0:T(8,128)S(1)}, bf16[8,72,128,128]{3,2,1,0:T(8,128)(...) while((s32[]{:T(128)}, f32[128,48,128]{2,1,0:T(8,128)}, ...), condition=%wide.region_3.4_spmd.clone, body=%wide.region_2.3_spmd.clone.sunk | while | flops 2192587264 | bytes 67635288 | solution.py:35
  402.4 7.4 bitcast_add_fusion.9
  422.3 7.4 bitcast_add_fusion.10
  462.4 7.4 bitcast_add_fusion.10
  502.4 7.4 bitcast_add_fusion.10
  542.5 7.4 bitcast_add_fusion.10
  582.5 7.4 bitcast_add_fusion.10
  622.6 7.4 bitcast_add_fusion.10
  662.6 7.4 bitcast_add_fusion.10
  678.9 159.5 %while.69 = (s32[]{:T(128)}, f32[128,48,128]{2,1,0:T(8,128)}, s32[8,72]{1,0:T(8,128)S(1)}, bf16[8,72,128,128]{3,2,1,0:T(8,128)(2,1)}, bf16[128,48,128]{2,1,0:T(8,128)(2,1)S(1)}, /*index=5*/s32[]{:T(128)}, s32[]{:T(128)}) while((s32[]{:T(128)}, f32[128,48,128]{2,1,0:T(8,128)}, s32[8,72]{1,0:T(8,128)S(1)}, ...), condition=%wide.region_6.7_spmd.clone, body=%wide.region_5.6_spmd.clone.sunk | while | flops 1096294016 | bytes 33818116 | solution.py:35
  711.1 7.4 bitcast_add_fusion.11
  731.1 7.4 bitcast_add_fusion.11
  751.1 7.4 bitcast_add_fusion.11
  771.1 7.4 bitcast_add_fusion.11
  791.1 7.4 bitcast_add_fusion.11
  811.0 7.4 bitcast_add_fusion.11
  831.0 7.4 bitcast_add_fusion.11
  849.3 85.6 %while.65 = (s32[]{:T(128)}, bf16[8,72,128,128]{3,2,1,0:T(8,128)(2,1)}, s32[8,72]{1,0:T(8,128)S(1)}, bf16[128,48,128]{2,1,0:T(8,128)(2,1)}, bf16[128,48,128]{2,1,0:T(8,128)(2,1)S(1)}, /*index=5*/s32[]{:T(128)}) while((s32[]{:T(128)}, bf16[8,72,128,128]{3,2,1,0:T(8,128)(2,1)}, s32[8,72]{1,0:T(8,128)S(1)}, bf16[128,48,128]{2,1,0:T(8,128)(2,1)}, ...), condition=%wide.region_9.10_spmd, body=%wide.region_8.9_spmd.sunk | while | flops 529669728 | bytes 40896072 | solution.py:143
  942.2 87.5 %while.66 = (s32[]{:T(128)}, bf16[8,72,128,128]{3,2,1,0:T(8,128)(2,1)}, s32[8,72]{1,0:T(8,128)S(1)}, bf16[128,48,128]{2,1,0:T(8,128)(2,1)}, bf16[128,48,128]{2,1...) while((s32[]{:T(128)}, bf16[8,72,128,128]{3,2,1,0:T(8,128)(2,1)}, s32[8,72]{1,0:T(8,128)S(1)}, ...), condition=%wide.region_12.13_spmd, body=%wide.region_11.12_spmd.sunk | while | flops 529669728 | bytes 34604596 | solution.py:105
  1029.8 31.7 %reduce-scatter.9.cloned.1.call-done = bf16[72,128,128]{2,1,0:T(8,128)(2,1)} async-done(((bf16[576,128,128]{2,1,0:T(8,128)(2,1)}), bf16[72,128,128]{2,1,0:T(8,128)(2,1)}) %reduce-scatter.9.cloned.1.call-update) | async-done | bytes 2359312 | tf_op jit(solution)/shard_map/reduce_scatter | solution.py:142
  1061.5 130.7 %reduce-scatter.11.cloned.1.call-done = bf16[72,128,128]{2,1,0:T(8,128)(2,1)} async-done(((bf16[576,128,128]{2,1,0:T(8,128)(2,1)}), bf16[72,128,128]{2,1,0:T(8,128)(2,1)}) %reduce-scatter.11.cloned.1.call-update) | async-done | bytes 2359312 | tf_op jit(solution)/shard_map/reduce_scatter | solution.py:104
  (339 shorter events, 686.1 us)
Async XLA Ops:
  7.2 2.9 copy-start.9
  7.2 3.0 copy-start.10
  7.2 42.2 %all-gather.9.cloned.1.call-start = ((), (), s32[]{:S(2)}) async-start(), calls=%async_computation.6 | async-start | bytes 1966080 | tf_op jit(solution)/shard_map/all_gather | solution.py:47
  7.9 78.9 %all-gather.11.cloned.1.call-start = ((), (), s32[]{:S(2)}) async-start(), calls=%async_computation.7 | async-start | bytes 1966080 | tf_op jit(solution)/shard_map/all_gather | solution.py:48
  8.7 177.5 %all-gather.7.cloned.1.call-start = ((), (), s32[]{:S(2)}) async-start(), calls=%async_computation.5 | async-start | bytes 21233664 | tf_op jit(solution)/shard_map/all_gather | solution.py:64
  9.4 342.0 %all-gather.5.cloned.1.call-start = ((), (), s32[]{:S(2)}) async-start(), calls=%async_computation.4 | async-start | bytes 21233664 | tf_op jit(solution)/shard_map/all_gather | solution.py:82
  10.0 1019.8 %reduce-scatter.5.cloned.1.call-start = ((), (), s32[]{:S(2)}) async-start(), calls=%async_computation.8 | async-start | bytes 1966080 | tf_op jit(solution)/shard_map/reduce_scatter | solution.py:87
  670.0 4.8 copy-start
  670.0 4.8 copy-start.3
  674.8 354.9 %reduce-scatter.7.cloned.1.call-start = ((), (), s32[]{:S(2)}) async-start(), calls=%async_computation.9 | async-start | bytes 1966080 | tf_op jit(solution)/shard_map/reduce_scatter | solution.py:126
  842.1 219.4 %reduce-scatter.9.cloned.1.call-start = ((), (), s32[]{:S(2)}) async-start(), calls=%async_computation.10 | async-start | bytes 21233664 | tf_op jit(solution)/shard_map/reduce_scatter | solution.py:142
  855.3 4.8 copy-start.8
  860.1 2.5 copy-start.6
  866.1 4.8 copy-start.8
  870.8 2.5 copy-start.6
  876.8 4.7 copy-start.8
  881.5 2.5 copy-start.6
  887.5 4.8 copy-start.8
  898.3 4.7 copy-start.8
  908.9 4.7 copy-start.8
  919.6 4.7 copy-start.8
  930.3 4.7 copy-start.8
  935.0 7.2 copy-start.1
  935.0 257.2 %reduce-scatter.11.cloned.1.call-start = ((), (), s32[]{:S(2)}) async-start(), calls=%async_computation.11 | async-start | bytes 21233664 | tf_op jit(solution)/shard_map/reduce_scatter | solution.py:104
  948.1 5.6 copy-start.2
  959.5 5.7 copy-start.2
  971.1 5.2 copy-start.2
  982.1 5.0 copy-start.2
  992.9 4.7 copy-start.2
  1003.5 4.9 copy-start.2
  1014.2 4.9 copy-start.2
  1024.9 4.8 copy-start.2
  (22 other events, 49.4 us)
Sparse Core Ops, SparseCore 0:
  9.6 39.7 all-gather.8
  50.9 35.8 all-gather.10
  88.7 97.4 all-gather.6
  188.0 98.5 all-gather.4
  675.0 35.5 reduce-scatter.4
  842.2 35.4 reduce-scatter.6
  935.1 126.3 reduce-scatter.8
  1065.7 126.4 reduce-scatter.10
where the time goes:
time: 1200 us
  matrix products  569 us (47%)
  waiting for transfers between devices  337 us (28%)
  local copies, waits for them, and re-layouts  264 us (22%)
  between operations  14.3 us (1%)
  other arithmetic  12.7 us (1%)
    dot_general x32, matrix products, place_add(): jnp.einsum('tnj,nc->tcj', product, onehot, precision=lax.Precision.HIGHEST)  233 us
    reduce_scatter x1, waiting for transfers between devices, shards(): lax.psum_scatter(lax.map(down_group_term, numbers).reshape(per_dev * lax....  131 us
    all_gather x1, waiting for transfers between devices, shards(): lax.all_gather(up_blocks, 'row', axis=1, tiled=True)[0]  97.6 us
    dot_general x64, matrix products, pick_blocks(): jnp.einsum('tcb,nc->tnb', tiles, onehot, preferred_element_type=jnp.float32)  74.6 us
    dot_general x8, local copies, waits for them, and re-layouts, up_step(): jnp.einsum('tnk,nkj->tnj', taken, blocks, preferred_element_type=jnp.floa...  49.6 us
    dot_general x8, local copies, waits for them, and re-layouts, back_step(): jnp.einsum('tnj,nkj->tnk', act_taken, blocks, preferred_element_type=jnp....  49.1 us
    dot_general x8, local copies, waits for them, and re-layouts, down_step(): jnp.einsum('tnk,nkj->tnj', hid_taken, blocks, preferred_element_type=jnp....  48.9 us
    dot_general x8, local copies, waits for them, and re-layouts, down_step(): jnp.einsum('tnj,nkj->tnk', cot_taken, blocks, preferred_element_type=jnp....  48.9 us
  transfers between devices with their start and end apart: 8, of which 5 were waited for; matrix products, arithmetic and copies ran while one was open for 43% of the time, Pallas kernels for 0%

commit v1 on v0

v1 whole, which is shorter than its diff:
```python
import functools
import math

import jax
import jax.numpy as jnp
from jax import lax
from jax.experimental import pallas as pl
from jax.experimental.pallas import tpu as pltpu
from jax.sharding import PartitionSpec as P

D = 6144
H = 24576
ANY = pl.BlockSpec(memory_space=pl.ANY)
VMEM = pl.BlockSpec(memory_space=pltpu.VMEM)
DOT = functools.partial(lax.dot_general, preferred_element_type=jnp.float32)


def split(count, least):
    for parts in (3, 2):
        if count % parts == 0 and count // parts >= least:
            return count // parts
    return count


def spmm(src, dst, owners, pieces, weights, groups, n_src, n_dst, flip):
    nb, side = weights[0].shape[0], weights[0].shape[-1]
    nw = len(weights)
    rows = max(r + p.shape[0] for p, r, _ in pieces)
    per = rows // groups
    width = n_dst * side
    chunk = split(nb, 8)
    unroll = next(u for u in (8, 6, 4, 3, 2, 1) if chunk % u == 0)
    places = [(r, c, p.shape) for p, r, c in pieces]
    np_ = len(places)
    dims = (((1,), (1 if flip else 0,)), ((), ()))

    def body(src_ref, dst_ref, own_ref, *refs):
        p_refs, w_refs = refs[:np_], refs[np_ : np_ + nw]
        outs = refs[np_ + nw : np_ + nw + groups]
        xs, ws, acc, sem_x, sem_w = refs[np_ + nw + groups :]
        loads = [
            pltpu.make_async_copy(
                ref, xs.at[pl.ds(r, shape[0]), pl.ds(c, shape[1])], sem_x.at[n]
            )
            for n, (ref, (r, c, shape)) in enumerate(zip(p_refs, places))
        ]
        for load in loads:
            load.start()
        steps = []
        for w in range(nw):
            for t in range(0, nb, chunk):
                copy = pltpu.make_async_copy(
                    w_refs[w].at[pl.ds(t, chunk)], ws.at[pl.ds(w * nb + t, chunk)], sem_w.at[len(steps)]
                )
                copy.start()
                steps.append((w, t, copy))
        outs[0][...] = jnp.zeros_like(outs[0])
        acc[...] = jnp.zeros_like(acc)
        for load in loads:
            load.wait()
        for w, t, copy in steps:
            copy.wait()
            first = own_ref[w] * nb + t

            def run(g, carry, w=w, t=t, first=first):
                for u in range(unroll):
                    n = g * unroll + u
                    i = src_ref[first + n]
                    j = dst_ref[first + n]
                    x = xs[:, pl.ds(pl.multiple_of(i * side, side), side)]
                    part = DOT(x, ws[w * nb + t + n], dims)
                    at = pl.ds(pl.multiple_of(j * side, side), side)
                    outs[0][:, at] += part[:per]
                    if groups > 1:
                        acc[:, at] += part[per:]
                return carry

            lax.fori_loop(0, chunk // unroll, run, 0)
        for g in range(1, groups):
            outs[g][...] = acc[pl.ds((g - 1) * per, per), :].astype(jnp.bfloat16)

    flops = 2 * rows * side * side * nb * nw
    return pl.pallas_call(
        body,
        grid_spec=pltpu.PrefetchScalarGridSpec(
            num_scalar_prefetch=3,
            grid=(),
            in_specs=[ANY] * (np_ + nw),
            out_specs=[VMEM] * groups,
            scratch_shapes=[
                pltpu.VMEM((rows, n_src * side), jnp.bfloat16),
                pltpu.VMEM((nw * nb, side, side), jnp.bfloat16),
                pltpu.VMEM((max(groups - 1, 1) * per, width), jnp.float32),
                pltpu.SemaphoreType.DMA((np_,)),
                pltpu.SemaphoreType.DMA((nw * (nb // chunk),)),
            ],
        ),
        out_shape=[jax.ShapeDtypeStruct((per, width), jnp.float32)]
        + [jax.ShapeDtypeStruct((per, width), jnp.bfloat16)] * (groups - 1),
        cost_estimate=pl.CostEstimate(
            flops=8 * flops, bytes_accessed=2 * nw * nb * side * side, transcendentals=0
        ),
    )(src, dst, owners, *[p for p, _, _ in pieces], *weights)


def outer(lidx, ridx, owners, left, right, adds, nb, side, n_left, n_right, factor):
    nw = owners.shape[0]
    rows = max(r + p.shape[0] for p, r, _ in left)
    chunk = split(nb, 8)
    unroll = next(u for u in (8, 6, 4, 3, 2, 1) if chunk % u == 0)
    l_places = [(r, c, p.shape) for p, r, c in left]
    r_places = [(r, c, p.shape) for p, r, c in right]
    nl, nr, na = len(left), len(right), len(adds)
    per_w = nb // chunk

    def body(l_ref, r_ref, own_ref, *refs):
        lp, rp, ap = refs[:nl], refs[nl : nl + nr], refs[nl + nr : nl + nr + na]
        outs = refs[nl + nr + na : nl + nr + na + nw]
        ls, lt, rs, os, sem_l, sem_r, sem_o, *more = refs[nl + nr + na + nw :]
        loads = []
        for buf, sem, p_refs, places in ((ls, sem_l, lp, l_places), (rs, sem_r, rp, r_places)):
            for n, (ref, (r, c, shape)) in enumerate(zip(p_refs, places)):
                loads.append(
                    pltpu.make_async_copy(ref, buf.at[pl.ds(r, shape[0]), pl.ds(c, shape[1])], sem.at[n])
                )
                loads[-1].start()
        gets = []
        if na:
            ad, sem_a = more
            for w in range(nw):
                gets.append(pltpu.make_async_copy(ap[w], ad.at[pl.ds(w * nb, nb)], sem_a.at[w]))
                gets[-1].start()
        for load in loads[:nl]:
            load.wait()

        def turn(c, carry):
            at = pl.multiple_of(c * side, side)
            lt[pl.ds(at, side), :] = ls[:, pl.ds(at, side)].T
            return carry

        lax.fori_loop(0, n_left, turn, 0)
        for load in loads[nl:]:
            load.wait()
        puts = []
        for w in range(nw):
            if na:
                gets[w].wait()
            for t in range(0, nb, chunk):
                first = own_ref[w] * nb + t

                def run(g, carry, w=w, t=t, first=first):
                    for u in range(unroll):
                        n = g * unroll + u
                        i = l_ref[first + n]
                        j = r_ref[first + n]
                        a = lt[pl.ds(pl.multiple_of(i * side, side), side), :]
                        b = rs[:, pl.ds(pl.multiple_of(j * side, side), side)]
                        got = DOT(a, b, (((1,), (0,)), ((), ()))) * factor
                        at = w * nb + t + n
                        if na:
                            got = got + ad[at].astype(jnp.float32)
                        os[at] = got.astype(jnp.bfloat16)
                    return carry

                lax.fori_loop(0, chunk // unroll, run, 0)
                put = pltpu.make_async_copy(
                    os.at[pl.ds(w * nb + t, chunk)], outs[w].at[pl.ds(t, chunk)], sem_o.at[len(puts)]
                )
                put.start()
                puts.append(put)
        for put in puts:
            put.wait()

    scratch = [
        pltpu.VMEM((rows, n_left * side), jnp.bfloat16),
        pltpu.VMEM((n_left * side, rows), jnp.bfloat16),
        pltpu.VMEM((rows, n_right * side), jnp.bfloat16),
        pltpu.VMEM((nw * nb, side, side), jnp.bfloat16),
        pltpu.SemaphoreType.DMA((nl,)),
        pltpu.SemaphoreType.DMA((nr,)),
        pltpu.SemaphoreType.DMA((nw * per_w,)),
    ]
    if na:
        scratch += [pltpu.VMEM((nw * nb, side, side), jnp.bfloat16), pltpu.SemaphoreType.DMA((nw,))]
    return pl.pallas_call(
        body,
        grid_spec=pltpu.PrefetchScalarGridSpec(
            num_scalar_prefetch=3,
            grid=(),
            in_specs=[ANY] * (nl + nr + na),
            out_specs=[ANY] * nw,
            scratch_shapes=scratch,
        ),
        out_shape=[jax.ShapeDtypeStruct((nb, side, side), jnp.bfloat16)] * nw,
        cost_estimate=pl.CostEstimate(
            flops=16 * rows * side * side * nb * nw, bytes_accessed=4 * nw * nb * side * side, transcendentals=0
        ),
    )(lidx, ridx, owners, *[p for p, _, _ in left], *[p for p, _, _ in right], *adds)


def solution(mesh):
    n_row, n_col = mesh.shape["row"], mesh.shape["col"]
    sizes = {"a": 2, "b": n_row // 4, "k": 2}

    def coords(r):
        return {"a": r // (2 * sizes["b"]), "b": (r // 2) % sizes["b"], "k": r % 2}

    def index(a, b, k):
        return (a * sizes["b"] + b) * 2 + k

    def shift(x, axis, s):
        pairs = []
        for r in range(n_row):
            at = coords(r)
            at[axis] = (at[axis] + s) % sizes[axis]
            pairs.append((r, index(**at)))
        return lax.ppermute(x, "row", pairs)

    def gather(x, axis):
        return [x] + [shift(x, axis, s) for s in range(1, sizes[axis])]

    def col_shift(x, s):
        return lax.ppermute(x, "col", [(z, (z + s) % n_col) for z in range(n_col)])

    def shards(inputs, up_cells, up_blocks, down_cells, down_blocks, cotangent):
        nb, side = up_blocks.shape[1], up_blocks.shape[-1]
        rows = inputs.shape[0]
        part = inputs.shape[1]
        in_blocks = D // side
        hid_blocks = H // (side * n_col)
        share = in_blocks // n_col
        factor = 1.0 / math.sqrt(rows * n_row)
        up, down = up_blocks[0], down_blocks[0]
        row, z = lax.axis_index("row"), lax.axis_index("col")
        here = {"a": row // (2 * sizes["b"]), "b": (row // 2) % sizes["b"], "k": row % 2}

        def owner(axis, off, dk):
            at = dict(here)
            at[axis] = (at[axis] + sizes[axis] - off) % sizes[axis]
            at["k"] = (at["k"] + dk) % 2
            return index(**at)

        def near(block):
            return (z - block // share + n_col) % n_col * share + block % share

        def far(block):
            return (block // share - z + n_col) % n_col * share + block % share

        up_in, up_hid = up_cells[0] // hid_blocks, up_cells[0] % hid_blocks
        down_hid, down_in = down_cells[0] // in_blocks, down_cells[0] % in_blocks
        up_from, up_to = near(up_in), far(up_in)
        down_from, down_to = near(down_in), far(down_in)
        up_own = [owner("a", s, dk) for dk in range(2) for s in range(sizes["a"])]
        down_own = [owner("b", s, dk) for dk in range(2) for s in range(sizes["b"])]
        up_owners, down_owners = jnp.stack(up_own), jnp.stack(down_own)

        up_near = gather(up, "a")
        down_near = gather(down, "b")
        up_all = up_near + [shift(w, "k", 1) for w in up_near]
        down_all = down_near + [shift(w, "k", 1) for w in down_near]

        def spread(x, axis):
            both = jnp.concatenate(gather(x, axis), axis=0)
            return [(p, 0, s * part) for s, p in enumerate([both] + [col_shift(both, s) for s in range(1, n_col)])]

        in_pieces = spread(inputs, "b")
        cot_pieces = spread(cotangent, "a")

        pre_own, *pre_send = spmm(
            up_from, up_hid, up_owners, in_pieces, up_all, sizes["b"], in_blocks, hid_blocks, False
        )
        hg_own, *hg_send = spmm(
            down_from, down_hid, down_owners, cot_pieces, down_all, sizes["a"], in_blocks, hid_blocks, True
        )

        def collect(own, others, axis):
            total = own
            for g, other in enumerate(others, 1):
                total = total + shift(other, axis, -g).astype(jnp.float32)
            return total

        preact = collect(pre_own, pre_send, "b")
        sig = jax.nn.sigmoid(preact)
        hidden = (preact * sig).astype(jnp.bfloat16)
        derivative = sig * (1.0 + preact * (1.0 - sig))
        act = (collect(hg_own, hg_send, "a") * derivative).astype(jnp.bfloat16)

        hid_pieces = [(p, s * rows, 0) for s, p in enumerate(gather(hidden, "a"))]
        act_pieces = [(p, s * rows, 0) for s, p in enumerate(gather(act, "b"))]

        out_own, *out_send = spmm(
            down_hid, down_to, down_owners, hid_pieces, down_all, sizes["a"], hid_blocks, in_blocks, False
        )
        in_own, *in_send = spmm(
            up_hid, up_to, up_owners, act_pieces, up_all, sizes["b"], hid_blocks, in_blocks, True
        )

        def scatter(own, others, axis):
            total = collect(own, others, axis)
            final = total[:, :part]
            for s in range(1, n_col):
                piece = total[:, s * part : (s + 1) * part].astype(jnp.bfloat16)
                final = final + col_shift(piece, s).astype(jnp.float32)
            return final.astype(jnp.bfloat16)

        output = scatter(out_own, out_send, "a")
        input_grad = scatter(in_own, in_send, "b")

        def weight_grad(lidx, ridx, owners, left, right, n_left, n_right, axis):
            n = sizes[axis]
            run = functools.partial(
                outer, lidx, ridx, nb=nb, side=side, n_left=n_left, n_right=n_right, factor=factor
            )
            theirs = run(owners=owners[n:], left=left, right=right, adds=[])
            got = [shift(t, "k", 1) for t in theirs]
            mine = run(owners=owners[:n], left=left, right=right, adds=got)
            total = mine[0].astype(jnp.float32)
            for s in range(1, n):
                total = total + shift(mine[s], axis, -s).astype(jnp.float32)
            return total.astype(jnp.bfloat16)[None]

        down_grad = weight_grad(
            down_hid, down_from, down_owners, hid_pieces, cot_pieces, hid_blocks, in_blocks, "b"
        )
        up_grad = weight_grad(
            up_from, up_hid, up_owners, in_pieces, act_pieces, in_blocks, hid_blocks, "a"
        )
        return output, input_grad, up_grad, down_grad

    in_specs = (
        P("row", "col"),
        P("col", None),
        P("col", "row", None, None),
        P("col", None),
        P("col", "row", None, None),
        P("row", "col"),
    )
    out_specs = (
        P("row", "col"),
        P("row", "col"),
        P("col", "row", None, None),
        P("col", "row", None, None),
    )
    return jax.shard_map(shards, mesh=mesh, in_specs=in_specs, out_specs=out_specs, check_vma=False)
```

time: 1200 us -> 476 us (0.40)
  matrix products: 569 us -> 0 us
  local copies, waits for them, and re-layouts: 264 us -> 6.77 us
  Pallas kernels: 0 us -> 138 us
  waiting for transfers between devices: 337 us -> 228 us
  starting transfers between devices: 0.31 us -> 73.7 us
  other arithmetic: 12.7 us -> 28.7 us
  between operations: 14.3 us -> 0.93 us
    dot_general x144 -> x0, matrix products: 569 us -> none  [the longest x32 233 us: place_add(): jnp.einsum('tnj,nc->tcj', product, onehot, precision=lax.Precision.HIGHEST)]
    dot_general x48 -> x0, local copies, waits for them, and re-layouts: 240 us -> none  [the longest x8 49.6 us: up_step(): jnp.einsum('tnk,nkj->tnj', taken, blocks, preferred_element_type=jnp.floa...]
    ppermute x0 -> x32, waiting for transfers between devices: none -> 228 us  [the longest x20 127 us: shift(): return lax.ppermute(x, 'row', pairs)]
    all_gather x4 -> x0, waiting for transfers between devices: 172 us -> none  [the longest x1 97.6 us: shards(): lax.all_gather(up_blocks, 'row', axis=1, tiled=True)[0]]
    reduce_scatter x4 -> x0, waiting for transfers between devices: 162 us -> none  [the longest x1 131 us: shards(): lax.psum_scatter(lax.map(down_group_term, numbers).reshape(per_dev * lax....]
    pallas_call x0 -> x8, Pallas kernels: none -> 138 us  [the longest x4 80.4 us: spmm(): pl.pallas_call(body, grid_spec=pltpu.PrefetchScalarGridSpec(num_scalar_pr...]
    ppermute x0 -> x32, starting transfers between devices: none -> 73.7 us  [the longest x12 54 us: col_shift(): return lax.ppermute(x, 'col', [(z, (z + s) % n_col) for z in range(n_col)])]
    another operation x4 -> x0, local copies, waits for them, and re-layouts: 14.5 us -> none
  transfers between devices with their start and end apart: 8 -> 32, of which waited for: 5 -> 11; matrix products, arithmetic and copies ran while one was open for 43% -> 5% of each run, Pallas kernels for 0% -> 29%
where the time goes in v1:
time: 476 us
  waiting for transfers between devices  228 us (48%)
  Pallas kernels  138 us (29%)
  starting transfers between devices  73.7 us (15%)
  other arithmetic  28.7 us (6%)
  local copies, waits for them, and re-layouts  6.77 us (1%)
    ppermute x20, waiting for transfers between devices, shift(): return lax.ppermute(x, 'row', pairs)  127 us
    ppermute x12, waiting for transfers between devices, col_shift(): return lax.ppermute(x, 'col', [(z, (z + s) % n_col) for z in range(n_col)])  101 us
    pallas_call x4, Pallas kernels, spmm(): pl.pallas_call(body, grid_spec=pltpu.PrefetchScalarGridSpec(num_scalar_pr...  80.4 us
    pallas_call x4, Pallas kernels, outer(): pl.pallas_call(body, grid_spec=pltpu.PrefetchScalarGridSpec(num_scalar_pr...  57.2 us
    ppermute x12, starting transfers between devices, col_shift(): return lax.ppermute(x, 'col', [(z, (z + s) % n_col) for z in range(n_col)])  54 us
    ppermute x20, starting transfers between devices, shift(): return lax.ppermute(x, 'row', pairs)  19.7 us
  transfers between devices with their start and end apart: 32, of which 11 were waited for; matrix products, arithmetic and copies ran while one was open for 5% of the time, Pallas kernels for 29%

profile of v1, /device:TPU:0, one launch (start us, length us, event | category | flops | bytes accessed | tf_op | source)
XLA Modules:
  0.0 475.6 jit_solution(9311019576765795783)
XLA Ops:
  0.6 3.0 collective-permute-start.9
  5.2 50.0 %collective-permute-done.9.refs_3_.refs_5_ = bf16[72,128,128]{2,1,0:T(8,128)(2,1)} collective-permute-done((bf16[72,128,128]{2,1,0:T(8,128)(2,1)}, bf16[72,128,128]{2,1,0:T(8,128)(2,1)}, u32[]{:S(2)}, u32[]{:S(2)}) %collective-permute-start.9) | collective-permute-done | bytes 2359328 | tf_op jit(solution)/shard_map/ppermute | solution.py:217
  59.5 7.5 %collective-permute-done.16 = bf16[128,1536]{1,0:T(8,128)(2,1)S(1)} collective-permute-done((bf16[128,1536]{1,0:T(8,128)(2,1)}, bf16[128,1536]{1,0:T(8,128)(2,1)S(1)}, u32[]{:S(2)}, u32[]{:S(2)}) %collective-permute-start.16) | collective-permute-done | bytes 393248 | tf_op jit(solution)/shard_map/ppermute | solution.py:217
  67.0 3.9 collective-permute-start.19
  75.1 13.8 %collective-permute-done.19.refs_3_.refs_5_ = bf16[256,1536]{1,0:T(8,128)(2,1)S(1)} collective-permute-done((bf16[256,1536]{1,0:T(8,128)(2,1)S(1)}, bf16[256,1536]{1,0:T(8,128)(2,1)S(1)}, u32[]{:S(2)}, u32[]{:S(2)}) %collective-permute-start.19) | collective-permute-done | bytes 786464 | tf_op jit(solution)/shard_map/ppermute | solution.py:223
  88.9 34.1 %collective-permute-start.17 = (bf16[256,1536]{1,0:T(8,128)(2,1)S(1)}, bf16[256,1536]{1,0:T(8,128)(2,1)S(1)}, u32[]{:S(2)}, u32[]{:S(2)}) collective-permute-start(bf16[256,1536]{1,0:T(8,128)(2,1)S(1)} %constant_dynamic-update-slice_fusion.2.refs_0_.refs_2_), channel_id=1, source_target_pairs={{0,1},{1,2},{2,3},{3,0},{4,5},{5,6},{6,7},{7,4},{8,9},{9,10},{10,1... | collective-permute-start | bytes 2359304 | tf_op jit(solution)/shard_map/ppermute | solution.py:223
  123.6 14.3 %collective-permute-done.18.refs_2_.refs_4_ = bf16[256,1536]{1,0:T(8,128)(2,1)S(1)} collective-permute-done((bf16[256,1536]{1,0:T(8,128)(2,1)S(1)}, bf16[256,1536]{1,0:T(8,128)(2,1)S(1)}, u32[]{:S(2)}, u32[]{:S(2)}) %collective-permute-start.18) | collective-permute-done | bytes 786464 | tf_op jit(solution)/shard_map/ppermute | solution.py:223
  141.6 2.0 collective-permute-start.1
  143.6 20.2 %shard_map.95 = (f32[128,6144]{1,0:T(8,128)}, bf16[128,6144]{1,0:T(8,128)(2,1)}) custom-call(s32[576]{0:T(1024)} %get-tuple-element.54.src_ref.r_ref, s32[576]{0:T(1024)} %get-tuple-element.55.src_ref.dst_ref.l_ref, s32[4]{0:T(128)} %pad_add_fusion.own_ref, bf16[256,1536]{1,0:T(8,128)(2,1)} %copy-done.5, bf16[256,1536]{1,0:T(8,128)(2,1)} %copy-done.10, ...), custom_call_target="tpu_custom_call" | custom-call | flops 19327352832 | bytes 9437184 | tf_op jit(solution)/shard_map/pallas_call | solution.py:83
  165.5 43.1 %collective-permute-done.2.refs_2_ = bf16[256,1536]{1,0:T(8,128)(2,1)} collective-permute-done((bf16[256,1536]{1,0:T(8,128)(2,1)S(1)}, bf16[256,1536]{1,0:T(8,128)(2,1)}, u32[]{:S(2)}, u32[]{:S(2)}) %collective-permute-start.2) | collective-permute-done | bytes 786464 | tf_op jit(solution)/shard_map/ppermute | solution.py:223
  208.7 20.0 %shard_map.93 = (f32[128,6144]{1,0:T(8,128)}, bf16[128,6144]{1,0:T(8,128)(2,1)}) custom-call(s32[576]{0:T(1024)} %get-tuple-element.53.src_ref.l_ref, s32[576]{0:T(1024)} %get-tuple-element.57.dst_ref.src_ref.r_ref, s32[4]{0:T(128)} %pad_add_fusion.1.own_ref, bf16[256,1536]{1,0:T(8,128)(2,1)} %copy-done.6, bf16[256,1536]{1,0:T(8,128)(2,1)} %collective-permute-done.1.refs_1_, ...), custom_call_target="tpu_custom_call" | custom-call | flops 19327352832 | bytes 9437184 | tf_op jit(solution)/shard_map/pallas_call | solution.py:83
  230.1 33.3 %collective-permute-done.7 = bf16[128,6144]{1,0:T(8,128)(2,1)S(1)} collective-permute-done((bf16[128,6144]{1,0:T(8,128)(2,1)}, bf16[128,6144]{1,0:T(8,128)(2,1)S(1)}, u32[]{:S(2)}, u32[]{:S(2)}) %collective-permute-start.7) | collective-permute-done | bytes 1572896 | tf_op jit(solution)/shard_map/ppermute | solution.py:217
  263.4 5.1 %multiply_convert_fusion = (bf16[128,6144]{1,0:T(8,128)(2,1)S(1)}, bf16[128,6144]{1,0:T(8,128)(2,1)}) fusion(f32[128,6144]{1,0:T(8,128)S(1)} %copy-done, bf16[128,6144]{1,0:T(8,128)(2,1)} %collective-permute-done.20, f32[128,6144]{1,0:T(8,128)} %get-tuple-element.20, bf16[128,6144]{1,0:T(8,128)(2,1)S(1)} %collective-permute-done.7), kind=kLoop, calls=%fused_computation.3 | loop fusion | flops 11796480 | bytes 12582912 | tf_op jit(solution)/shard_map/convert_element_type | solution.py:286
  275.0 28.3 %collective-permute-done.21.refs_1_.refs_5_ = bf16[128,6144]{1,0:T(8,128)(2,1)S(1)} collective-permute-done((bf16[128,6144]{1,0:T(8,128)(2,1)S(1)}, bf16[128,6144]{1,0:T(8,128)(2,1)S(1)}, u32[]{:S(2)}, u32[]{:S(2)}) %collective-permute-start.21) | collective-permute-done | bytes 1572896 | tf_op jit(solution)/shard_map/ppermute | solution.py:217
  304.5 20.3 %shard_map.96 = (f32[128,6144]{1,0:T(8,128)}, bf16[128,6144]{1,0:T(8,128)(2,1)}) custom-call(s32[576]{0:T(1024)} %get-tuple-element.57.dst_ref.src_ref.r_ref, s32[576]{0:T(1024)} %get-tuple-element.52.dst_ref, s32[4]{0:T(128)} %pad_add_fusion.1.own_ref, bf16[128,6144]{1,0:T(8,128)(2,1)} %copy-done.3, bf16[128,6144]{1,0:T(8,128)(2,1)} %copy-done.7, ...), custom_call_target="tpu_custom_call" | custom-call | flops 19327352832 | bytes 9437184 | tf_op jit(solution)/shard_map/pallas_call | solution.py:83
  326.3 19.8 %shard_map.94 = (f32[128,6144]{1,0:T(8,128)}, bf16[128,6144]{1,0:T(8,128)(2,1)}) custom-call(s32[576]{0:T(1024)} %get-tuple-element.55.src_ref.dst_ref.l_ref, s32[576]{0:T(1024)} %get-tuple-element.56.dst_ref, s32[4]{0:T(128)} %pad_add_fusion.own_ref, bf16[128,6144]{1,0:T(8,128)(2,1)} %get-tuple-element.45.refs_0_, ...), custom_call_target="tpu_custom_call" | custom-call | flops 19327352832 | bytes 9437184 | tf_op jit(solution)/shard_map/pallas_call | solution.py:83
  347.5 14.0 %shard_map.99 = (bf16[72,128,128]{2,1,0:T(8,128)(2,1)}, bf16[72,128,128]{2,1,0:T(8,128)(2,1)}) custom-call(s32[576]{0:T(1024)} %get-tuple-element.55.src_ref.dst_ref.l_ref, s32[576]{0:T(1024)} %get-tuple-element.54.src_ref.r_ref, s32[2]{0:T(128)} %pad_add_fusion.5.own_ref, bf16[128,6144]{1,0:T(8,128)(2,1)} %get-tuple-element.45.refs_0_, ...), custom_call_target="tpu_custom_call" | custom-call | flops 9663676416 | bytes 9437184 | tf_op jit(solution)/shard_map/pallas_call | solution.py:185
  362.1 13.9 %shard_map.97 = (bf16[72,128,128]{2,1,0:T(8,128)(2,1)}, bf16[72,128,128]{2,1,0:T(8,128)(2,1)}) custom-call(s32[576]{0:T(1024)} %get-tuple-element.53.src_ref.l_ref, s32[576]{0:T(1024)} %get-tuple-element.57.dst_ref.src_ref.r_ref, s32[2]{0:T(128)} %pad_add_fusion.3.own_ref, bf16[256,1536]{1,0:T(8,128)(2,1)} %copy-done.6, ...), custom_call_target="tpu_custom_call" | custom-call | flops 9663676416 | bytes 9437184 | tf_op jit(solution)/shard_map/pallas_call | solution.py:185
  377.4 2.8 fusion.22
  381.2 5.1 %collective-permute-start.23 = (bf16[128,1536]{1,0:T(8,128)(2,1)}, bf16[128,1536]{1,0:T(8,128)(2,1)S(1)}, u32[]{:S(2)}, u32[]{:S(2)}) collective-permute-start(bf16[128,1536]{1,0:T(8,128)(2,1)} %get-tuple-element.46), channel_id=1, source_target_pairs={{0,1},{1,2},{2,3},{3,0},{4,5},{5,6},{6,7},{7,4},{8,9},{9,10},{10,1... | collective-permute-start | bytes 1179656 | tf_op jit(solution)/shard_map/ppermute | solution.py:223
  386.3 14.8 %shard_map.100 = (bf16[72,128,128]{2,1,0:T(8,128)(2,1)}, bf16[72,128,128]{2,1,0:T(8,128)(2,1)}) custom-call(s32[576]{0:T(1024)} %get-tuple-element.55.src_ref.dst_ref.l_ref, s32[576]{0:T(1024)} %get-tuple-element.54.src_ref.r_ref, s32[2]{0:T(128)} %pad_add_fusion.4.own_ref, bf16[128,6144]{1,0:T(8,128)(2,1)} %get-tuple-element.45.refs_0_, ...), custom_call_target="tpu_custom_call" | custom-call | flops 9663676416 | bytes 9437184 | tf_op jit(solution)/shard_map/pallas_call | solution.py:185
  401.1 4.0 collective-permute-start.24
  405.7 14.5 %shard_map.98 = (bf16[72,128,128]{2,1,0:T(8,128)(2,1)}, bf16[72,128,128]{2,1,0:T(8,128)(2,1)}) custom-call(s32[576]{0:T(1024)} %get-tuple-element.53.src_ref.l_ref, s32[576]{0:T(1024)} %get-tuple-element.57.dst_ref.src_ref.r_ref, s32[2]{0:T(128)} %pad_add_fusion.2.own_ref, bf16[256,1536]{1,0:T(8,128)(2,1)} %copy-done.6, ...), custom_call_target="tpu_custom_call" | custom-call | flops 9663676416 | bytes 9437184 | tf_op jit(solution)/shard_map/pallas_call | solution.py:185
  421.0 2.8 fusion.23
  424.0 3.7 collective-permute-start.15
  427.8 2.2 fusion.4
  430.0 7.8 %collective-permute-done.13 = bf16[128,1536]{1,0:T(8,128)(2,1)S(1)} collective-permute-done((bf16[128,1536]{1,0:T(8,128)(2,1)S(1)}, bf16[128,1536]{1,0:T(8,128)(2,1)S(1)}, u32[]{:S(2)}, u32[]{:S(2)}) %collective-permute-start.13) | collective-permute-done | bytes 393248 | tf_op jit(solution)/shard_map/ppermute | solution.py:223
  437.7 5.9 %collective-permute-done.15 = bf16[128,1536]{1,0:T(8,128)(2,1)S(1)} collective-permute-done((bf16[128,1536]{1,0:T(8,128)(2,1)S(1)}, bf16[128,1536]{1,0:T(8,128)(2,1)S(1)}, u32[]{:S(2)}, u32[]{:S(2)}) %collective-permute-start.15) | collective-permute-done | bytes 393248 | tf_op jit(solution)/shard_map/ppermute | solution.py:223
  443.6 15.7 %collective-permute-done.14 = bf16[128,1536]{1,0:T(8,128)(2,1)S(1)} collective-permute-done((bf16[128,1536]{1,0:T(8,128)(2,1)S(1)}, bf16[128,1536]{1,0:T(8,128)(2,1)S(1)}, u32[]{:S(2)}, u32[]{:S(2)}) %collective-permute-start.14) | collective-permute-done | bytes 393248 | tf_op jit(solution)/shard_map/ppermute | solution.py:223
  460.3 4.5 fusion.1
  464.8 8.1 %collective-permute-done.28 = bf16[72,128,128]{2,1,0:T(8,128)(2,1)S(1)} collective-permute-done((bf16[72,128,128]{2,1,0:T(8,128)(2,1)}, bf16[72,128,128]{2,1,0:T(8,128)(2,1)S(1)}, u32[]{:S(2)}, u32[]{:S(2)}) %collective-permute-start.28) | collective-permute-done | bytes 2359328 | tf_op jit(solution)/shard_map/ppermute | solution.py:217
  472.9 2.7 fusion
  (89 shorter events, 33.4 us)
Async XLA Ops:
  0.6 54.6 %collective-permute-start.9 = (bf16[72,128,128]{2,1,0:T(8,128)(2,1)}, bf16[72,128,128]{2,1,0:T(8,128)(2,1)}, u32[]{:S(2)}, u32[]{:S(2)}) collective-permute-start(bf16[72,128,128]{2,1,0:T(8,128)(2,1)} %bitcast.18), channel_id=1, source_target_pairs={{0,8},{4,12},{8,0},{12,4},{16,24},{20,28},{24,16},{28,20},{1,9},{5... | collective-permute-start | bytes 7077896 | tf_op jit(solution)/shard_map/ppermute | solution.py:217
  3.7 134.3 %collective-permute-start.4 = (bf16[72,128,128]{2,1,0:T(8,128)(2,1)}, bf16[72,128,128]{2,1,0:T(8,128)(2,1)}, u32[]{:S(2)}, u32[]{:S(2)}) collective-permute-start(bf16[72,128,128]{2,1,0:T(8,128)(2,1)} %bitcast.14), channel_id=1, source_target_pairs={{0,16},{4,20},{8,24},{12,28},{16,0},{20,4},{24,8},{28,12},{1,17},{... | collective-permute-start | bytes 7077896 | tf_op jit(solution)/shard_map/ppermute | solution.py:217
  5.2 135.4 %collective-permute-start.10 = (bf16[72,128,128]{2,1,0:T(8,128)(2,1)}, bf16[72,128,128]{2,1,0:T(8,128)(2,1)}, u32[]{:S(2)}, u32[]{:S(2)}) collective-permute-start(bf16[72,128,128]{2,1,0:T(8,128)(2,1)} %bitcast.19), channel_id=1, source_target_pairs={{0,4},{4,0},{8,12},{12,8},{16,20},{20,16},{24,28},{28,24},{1,5},{5... | collective-permute-start | bytes 7077896 | tf_op jit(solution)/shard_map/ppermute | solution.py:217
  55.2 86.4 %collective-permute-start.11 = (bf16[72,128,128]{2,1,0:T(8,128)(2,1)}, bf16[72,128,128]{2,1,0:T(8,128)(2,1)}, u32[]{:S(2)}, u32[]{:S(2)}) collective-permute-start(bf16[72,128,128]{2,1,0:T(8,128)(2,1)} %collective-permute-done.9.refs_3_.refs_5_), channel_id=1, source_target_pairs={{0,4},{4,0},{8,12},{12,8},{16,20},{20,16},{24,28},{28,24},{1,5},{5... | collective-permute-start | bytes 7077896 | tf_op jit(solution)/shard_map/ppermute | solution.py:217
  55.2 11.8 %collective-permute-start.16 = (bf16[128,1536]{1,0:T(8,128)(2,1)}, bf16[128,1536]{1,0:T(8,128)(2,1)S(1)}, u32[]{:S(2)}, u32[]{:S(2)}) collective-permute-start(bf16[128,1536]{1,0:T(8,128)(2,1)} %param.11), channel_id=1, source_target_pairs={{0,16},{4,20},{8,24},{12,28},{16,0},{20,4},{24,8},{28,12},{1,17},{... | collective-permute-start | bytes 1179656 | tf_op jit(solution)/shard_map/ppermute | solution.py:217
  57.0 15.3 %collective-permute-start = (bf16[128,1536]{1,0:T(8,128)(2,1)}, bf16[128,1536]{1,0:T(8,128)(2,1)S(1)}, u32[]{:S(2)}, u32[]{:S(2)}) collective-permute-start(bf16[128,1536]{1,0:T(8,128)(2,1)} %param.6), channel_id=1, source_target_pairs={{0,8},{4,12},{8,0},{12,4},{16,24},{20,28},{24,16},{28,20},{1,9},{5... | collective-permute-start | bytes 1179656 | tf_op jit(solution)/shard_map/ppermute | solution.py:217
  67.0 21.9 %collective-permute-start.19 = (bf16[256,1536]{1,0:T(8,128)(2,1)S(1)}, bf16[256,1536]{1,0:T(8,128)(2,1)S(1)}, u32[]{:S(2)}, u32[]{:S(2)}) collective-permute-start(bf16[256,1536]{1,0:T(8,128)(2,1)S(1)} %constant_dynamic-update-slice_fusion.2.refs_0_.refs_2_), channel_id=1, source_target_pairs={{0,3},{1,0},{2,1},{3,2},{4,7},{5,4},{6,5},{7,6},{8,11},{9,8},{10,9... | collective-permute-start | bytes 2359304 | tf_op jit(solution)/shard_map/ppermute | solution.py:223
  72.3 65.6 %collective-permute-start.18 = (bf16[256,1536]{1,0:T(8,128)(2,1)S(1)}, bf16[256,1536]{1,0:T(8,128)(2,1)S(1)}, u32[]{:S(2)}, u32[]{:S(2)}) collective-permute-start(bf16[256,1536]{1,0:T(8,128)(2,1)S(1)} %constant_dynamic-update-slice_fusion.2.refs_0_.refs_2_), channel_id=1, source_target_pairs={{0,2},{1,3},{2,0},{3,1},{4,6},{5,7},{6,4},{7,5},{8,10},{9,11},{10,... | collective-permute-start | bytes 2359304 | tf_op jit(solution)/shard_map/ppermute | solution.py:223
  88.9 51.6 %collective-permute-start.17 = (bf16[256,1536]{1,0:T(8,128)(2,1)S(1)}, bf16[256,1536]{1,0:T(8,128)(2,1)S(1)}, u32[]{:S(2)}, u32[]{:S(2)}) collective-permute-start(bf16[256,1536]{1,0:T(8,128)(2,1)S(1)} %constant_dynamic-update-slice_fusion.2.refs_0_.refs_2_), channel_id=1, source_target_pairs={{0,1},{1,2},{2,3},{3,0},{4,5},{5,6},{6,7},{7,4},{8,9},{9,10},{10,1... | collective-permute-start | bytes 2359304 | tf_op jit(solution)/shard_map/ppermute | solution.py:223
  138.0 70.7 %collective-permute-start.5 = (bf16[72,128,128]{2,1,0:T(8,128)(2,1)}, bf16[72,128,128]{2,1,0:T(8,128)(2,1)}, u32[]{:S(2)}, u32[]{:S(2)}) collective-permute-start(bf16[72,128,128]{2,1,0:T(8,128)(2,1)} %bitcast.15), channel_id=1, source_target_pairs={{0,4},{4,0},{8,12},{12,8},{16,20},{20,16},{24,28},{28,24},{1,5},{5... | collective-permute-start | bytes 7077896 | tf_op jit(solution)/shard_map/ppermute | solution.py:217
  138.0 70.7 %collective-permute-start.6 = (bf16[72,128,128]{2,1,0:T(8,128)(2,1)}, bf16[72,128,128]{2,1,0:T(8,128)(2,1)}, u32[]{:S(2)}, u32[]{:S(2)}) collective-permute-start(bf16[72,128,128]{2,1,0:T(8,128)(2,1)} %collective-permute-done.4.refs_5_.refs_3_), channel_id=1, source_target_pairs={{0,4},{4,0},{8,12},{12,8},{16,20},{20,16},{24,28},{28,24},{1,5},{5... | collective-permute-start | bytes 7077896 | tf_op jit(solution)/shard_map/ppermute | solution.py:217
  140.5 23.3 %collective-permute-start.3 = (bf16[256,1536]{1,0:T(8,128)(2,1)S(1)}, bf16[256,1536]{1,0:T(8,128)(2,1)S(1)}, u32[]{:S(2)}, u32[]{:S(2)}) collective-permute-start(bf16[256,1536]{1,0:T(8,128)(2,1)S(1)} %constant_dynamic-update-slice_fusion.refs_0_), channel_id=1, source_target_pairs={{0,3},{1,0},{2,1},{3,2},{4,7},{5,4},{6,5},{7,6},{8,11},{9,8},{10,9... | collective-permute-start | bytes 2359304 | tf_op jit(solution)/shard_map/ppermute | solution.py:223
  140.6 68.1 %collective-permute-start.2 = (bf16[256,1536]{1,0:T(8,128)(2,1)S(1)}, bf16[256,1536]{1,0:T(8,128)(2,1)}, u32[]{:S(2)}, u32[]{:S(2)}) collective-permute-start(bf16[256,1536]{1,0:T(8,128)(2,1)S(1)} %constant_dynamic-update-slice_fusion.refs_0_), channel_id=1, source_target_pairs={{0,2},{1,3},{2,0},{3,1},{4,6},{5,7},{6,4},{7,5},{8,10},{9,11},{10,... | collective-permute-start | bytes 2359304 | tf_op jit(solution)/shard_map/ppermute | solution.py:223
  141.6 67.1 %collective-permute-start.1 = (bf16[256,1536]{1,0:T(8,128)(2,1)S(1)}, bf16[256,1536]{1,0:T(8,128)(2,1)}, u32[]{:S(2)}, u32[]{:S(2)}) collective-permute-start(bf16[256,1536]{1,0:T(8,128)(2,1)S(1)} %constant_dynamic-update-slice_fusion.refs_0_), channel_id=1, source_target_pairs={{0,1},{1,2},{2,3},{3,0},{4,5},{5,6},{6,7},{7,4},{8,9},{9,10},{10,1... | collective-permute-start | bytes 2359304 | tf_op jit(solution)/shard_map/ppermute | solution.py:223
  163.8 66.3 %collective-permute-start.20 = (bf16[128,6144]{1,0:T(8,128)(2,1)}, bf16[128,6144]{1,0:T(8,128)(2,1)}, u32[]{:S(2)}, u32[]{:S(2)}) collective-permute-start(bf16[128,6144]{1,0:T(8,128)(2,1)} %get-tuple-element.25), channel_id=1, source_target_pairs={{0,16},{4,20},{8,24},{12,28},{16,0},{20,4},{24,8},{28,12},{1,17},{... | collective-permute-start | bytes 4718600 | tf_op jit(solution)/shard_map/ppermute | solution.py:217
  228.7 34.8 %collective-permute-start.7 = (bf16[128,6144]{1,0:T(8,128)(2,1)}, bf16[128,6144]{1,0:T(8,128)(2,1)S(1)}, u32[]{:S(2)}, u32[]{:S(2)}) collective-permute-start(bf16[128,6144]{1,0:T(8,128)(2,1)} %get-tuple-element.21), channel_id=1, source_target_pairs={{0,8},{4,12},{8,0},{12,4},{16,24},{20,28},{24,16},{28,20},{1,9},{5... | collective-permute-start | bytes 4718600 | tf_op jit(solution)/shard_map/ppermute | solution.py:217
  269.7 33.6 %collective-permute-start.21 = (bf16[128,6144]{1,0:T(8,128)(2,1)S(1)}, bf16[128,6144]{1,0:T(8,128)(2,1)S(1)}, u32[]{:S(2)}, u32[]{:S(2)}) collective-permute-start(bf16[128,6144]{1,0:T(8,128)(2,1)S(1)} %get-tuple-element.44.refs_0_.refs_4_), channel_id=1, source_target_pairs={{0,8},{4,12},{8,0},{12,4},{16,24},{20,28},{24,16},{28,20},{1,9},{5... | collective-permute-start | bytes 4718600 | tf_op jit(solution)/shard_map/ppermute | solution.py:217
  273.5 52.8 %collective-permute-start.8 = (bf16[128,6144]{1,0:T(8,128)(2,1)}, bf16[128,6144]{1,0:T(8,128)(2,1)}, u32[]{:S(2)}, u32[]{:S(2)}) collective-permute-start(bf16[128,6144]{1,0:T(8,128)(2,1)} %get-tuple-element.45.refs_0_), channel_id=1, source_target_pairs={{0,16},{4,20},{8,24},{12,28},{16,0},{20,4},{24,8},{28,12},{1,17},{... | collective-permute-start | bytes 4718600 | tf_op jit(solution)/shard_map/ppermute | solution.py:217
  324.9 51.3 %collective-permute-start.22 = (bf16[128,6144]{1,0:T(8,128)(2,1)}, bf16[128,6144]{1,0:T(8,128)(2,1)S(1)}, u32[]{:S(2)}, u32[]{:S(2)}) collective-permute-start(bf16[128,6144]{1,0:T(8,128)(2,1)} %get-tuple-element.27), channel_id=1, source_target_pairs={{0,8},{4,12},{8,0},{12,4},{16,24},{20,28},{24,16},{28,20},{1,9},{5... | collective-permute-start | bytes 4718600 | tf_op jit(solution)/shard_map/ppermute | solution.py:217
  346.2 74.0 %collective-permute-start.12 = (bf16[128,6144]{1,0:T(8,128)(2,1)}, bf16[128,6144]{1,0:T(8,128)(2,1)}, u32[]{:S(2)}, u32[]{:S(2)}) collective-permute-start(bf16[128,6144]{1,0:T(8,128)(2,1)} %get-tuple-element.23), channel_id=1, source_target_pairs={{0,16},{4,20},{8,24},{12,28},{16,0},{20,4},{24,8},{28,12},{1,17},{... | collective-permute-start | bytes 4718600 | tf_op jit(solution)/shard_map/ppermute | solution.py:217
  361.6 19.7 %collective-permute-start.29 = (bf16[72,128,128]{2,1,0:T(8,128)(2,1)}, bf16[72,128,128]{2,1,0:T(8,128)(2,1)}, u32[]{:S(2)}, u32[]{:S(2)}) collective-permute-start(bf16[72,128,128]{2,1,0:T(8,128)(2,1)} %get-tuple-element.32), channel_id=1, source_target_pairs={{0,4},{4,0},{8,12},{12,8},{16,20},{20,16},{24,28},{28,24},{1,5},{5... | collective-permute-start | bytes 7077896 | tf_op jit(solution)/shard_map/ppermute | solution.py:217
  361.6 24.6 %collective-permute-start.30 = (bf16[72,128,128]{2,1,0:T(8,128)(2,1)}, bf16[72,128,128]{2,1,0:T(8,128)(2,1)}, u32[]{:S(2)}, u32[]{:S(2)}) collective-permute-start(bf16[72,128,128]{2,1,0:T(8,128)(2,1)} %get-tuple-element.33), channel_id=1, source_target_pairs={{0,4},{4,0},{8,12},{12,8},{16,20},{20,16},{24,28},{28,24},{1,5},{5... | collective-permute-start | bytes 7077896 | tf_op jit(solution)/shard_map/ppermute | solution.py:217
  376.0 25.0 %collective-permute-start.26 = (bf16[72,128,128]{2,1,0:T(8,128)(2,1)}, bf16[72,128,128]{2,1,0:T(8,128)(2,1)}, u32[]{:S(2)}, u32[]{:S(2)}) collective-permute-start(bf16[72,128,128]{2,1,0:T(8,128)(2,1)} %get-tuple-element.28), channel_id=1, source_target_pairs={{0,4},{4,0},{8,12},{12,8},{16,20},{20,16},{24,28},{28,24},{1,5},{5... | collective-permute-start | bytes 7077896 | tf_op jit(solution)/shard_map/ppermute | solution.py:217
  376.2 28.9 %collective-permute-start.27 = (bf16[72,128,128]{2,1,0:T(8,128)(2,1)}, bf16[72,128,128]{2,1,0:T(8,128)(2,1)}, u32[]{:S(2)}, u32[]{:S(2)}) collective-permute-start(bf16[72,128,128]{2,1,0:T(8,128)(2,1)} %get-tuple-element.29), channel_id=1, source_target_pairs={{0,4},{4,0},{8,12},{12,8},{16,20},{20,16},{24,28},{28,24},{1,5},{5... | collective-permute-start | bytes 7077896 | tf_op jit(solution)/shard_map/ppermute | solution.py:217
  381.2 42.7 %collective-permute-start.23 = (bf16[128,1536]{1,0:T(8,128)(2,1)}, bf16[128,1536]{1,0:T(8,128)(2,1)S(1)}, u32[]{:S(2)}, u32[]{:S(2)}) collective-permute-start(bf16[128,1536]{1,0:T(8,128)(2,1)} %get-tuple-element.46), channel_id=1, source_target_pairs={{0,1},{1,2},{2,3},{3,0},{4,5},{5,6},{6,7},{7,4},{8,9},{9,10},{10,1... | collective-permute-start | bytes 1179656 | tf_op jit(solution)/shard_map/ppermute | solution.py:223
  386.3 37.8 %collective-permute-start.25 = (bf16[128,1536]{1,0:T(8,128)(2,1)}, bf16[128,1536]{1,0:T(8,128)(2,1)}, u32[]{:S(2)}, u32[]{:S(2)}) collective-permute-start(bf16[128,1536]{1,0:T(8,128)(2,1)} %get-tuple-element.47), channel_id=1, source_target_pairs={{0,3},{1,0},{2,1},{3,2},{4,7},{5,4},{6,5},{7,6},{8,11},{9,8},{10,9... | collective-permute-start | bytes 1179656 | tf_op jit(solution)/shard_map/ppermute | solution.py:223
  401.1 26.7 %collective-permute-start.24 = (bf16[128,1536]{1,0:T(8,128)(2,1)}, bf16[128,1536]{1,0:T(8,128)(2,1)}, u32[]{:S(2)}, u32[]{:S(2)}) collective-permute-start(bf16[128,1536]{1,0:T(8,128)(2,1)} %get-tuple-element.48), channel_id=1, source_target_pairs={{0,2},{1,3},{2,0},{3,1},{4,6},{5,7},{6,4},{7,5},{8,10},{9,11},{10,... | collective-permute-start | bytes 1179656 | tf_op jit(solution)/shard_map/ppermute | solution.py:223
  405.1 55.2 %collective-permute-start.31 = (bf16[72,128,128]{2,1,0:T(8,128)(2,1)}, bf16[72,128,128]{2,1,0:T(8,128)(2,1)}, u32[]{:S(2)}, u32[]{:S(2)}) collective-permute-start(bf16[72,128,128]{2,1,0:T(8,128)(2,1)} %get-tuple-element.35), channel_id=1, source_target_pairs={{0,8},{4,12},{8,0},{12,4},{16,24},{20,28},{24,16},{28,20},{1,9},{5... | collective-permute-start | bytes 7077896 | tf_op jit(solution)/shard_map/ppermute | solution.py:217
  420.2 52.7 %collective-permute-start.28 = (bf16[72,128,128]{2,1,0:T(8,128)(2,1)}, bf16[72,128,128]{2,1,0:T(8,128)(2,1)S(1)}, u32[]{:S(2)}, u32[]{:S(2)}) collective-permute-start(bf16[72,128,128]{2,1,0:T(8,128)(2,1)} %get-tuple-element.31), channel_id=1, source_target_pairs={{0,16},{4,20},{8,24},{12,28},{16,0},{20,4},{24,8},{28,12},{1,17},{... | collective-permute-start | bytes 7077896 | tf_op jit(solution)/shard_map/ppermute | solution.py:217
  423.9 13.8 %collective-permute-start.13 = (bf16[128,1536]{1,0:T(8,128)(2,1)S(1)}, bf16[128,1536]{1,0:T(8,128)(2,1)S(1)}, u32[]{:S(2)}, u32[]{:S(2)}) collective-permute-start(bf16[128,1536]{1,0:T(8,128)(2,1)S(1)} %get-tuple-element.49), channel_id=1, source_target_pairs={{0,1},{1,2},{2,3},{3,0},{4,5},{5,6},{6,7},{7,4},{8,9},{9,10},{10,1... | collective-permute-start | bytes 1179656 | tf_op jit(solution)/shard_map/ppermute | solution.py:223
  424.0 19.6 %collective-permute-start.15 = (bf16[128,1536]{1,0:T(8,128)(2,1)S(1)}, bf16[128,1536]{1,0:T(8,128)(2,1)S(1)}, u32[]{:S(2)}, u32[]{:S(2)}) collective-permute-start(bf16[128,1536]{1,0:T(8,128)(2,1)S(1)} %get-tuple-element.50), channel_id=1, source_target_pairs={{0,3},{1,0},{2,1},{3,2},{4,7},{5,4},{6,5},{7,6},{8,11},{9,8},{10,9... | collective-permute-start | bytes 1179656 | tf_op jit(solution)/shard_map/ppermute | solution.py:223
  427.8 31.6 %collective-permute-start.14 = (bf16[128,1536]{1,0:T(8,128)(2,1)S(1)}, bf16[128,1536]{1,0:T(8,128)(2,1)S(1)}, u32[]{:S(2)}, u32[]{:S(2)}) collective-permute-start(bf16[128,1536]{1,0:T(8,128)(2,1)S(1)} %get-tuple-element.51), channel_id=1, source_target_pairs={{0,2},{1,3},{2,0},{3,1},{4,6},{5,7},{6,4},{7,5},{8,10},{9,11},{10,... | collective-permute-start | bytes 1179656 | tf_op jit(solution)/shard_map/ppermute | solution.py:223
  (12 other events, 304.8 us)
